TPU v7x, 32 devices: a whole 2x2x4 slice. The times are simulated.
32 devices in a mesh: fsdp: 4 (over y, x), seq: 8 (over z, core).
Axes of the slice: x: 2, y: 2, z: 4, core: 2. Of those that a mesh axis runs over, the one named last changes fastest.
Arguments:
- tokens: bfloat16 [8, 1024, 2048], P('fsdp', 'seq'), may hold values from -6 to 6
- positions: int32 [8, 1024], P('fsdp', 'seq'), may hold values from 0 to 2046, as said below
- gain_attn: bfloat16 [2048], P('fsdp'), may hold values from 0.099609375 to 1.8984375
- w_query: bfloat16 [2048, 2048], P('fsdp'), may hold values from -0.1875 to 0.1875
- w_key: bfloat16 [2048, 512], P('fsdp'), may hold values from -0.1875 to 0.1875
- w_value: bfloat16 [2048, 512], P('fsdp'), may hold values from -0.125 to 0.125
- w_out: bfloat16 [2048, 2048], P('fsdp'), may hold values from -0.5 to 0.5
- gain_ffn: bfloat16 [2048], P('fsdp'), may hold values from 0.099609375 to 1.8984375
- w_gate: bfloat16 [2048, 8192], P('fsdp'), may hold values from -0.125 to 0.125
- w_up: bfloat16 [2048, 8192], P('fsdp'), may hold values from -0.125 to 0.125
- w_down: bfloat16 [8192, 2048], P('fsdp'), may hold values from -0.0625 to 0.0625
- grad_out: bfloat16 [8, 1024, 2048], P('fsdp', 'seq'), may hold values from -6 to 6
Outputs:
- layer_out: bfloat16 [8, 1024, 2048], P('fsdp', 'seq')
- grad_tokens: bfloat16 [8, 1024, 2048], P('fsdp', 'seq')
- grad_gain_attn: float32 [2048], P('fsdp')
- grad_w_query: float32 [2048, 2048], P('fsdp')
- grad_w_key: float32 [2048, 512], P('fsdp')
- grad_w_value: float32 [2048, 512], P('fsdp')
- grad_w_out: float32 [2048, 2048], P('fsdp')
- grad_gain_ffn: float32 [2048], P('fsdp')
- grad_w_gate: float32 [2048, 8192], P('fsdp')
- grad_w_up: float32 [2048, 8192], P('fsdp')
- grad_w_down: float32 [8192, 2048], P('fsdp')
Inputs may be any that keep to these rules, and one draw needn't show every extreme that they name: Along each sequence the positions rise strictly, by 1 or 2 from one token to the next.
All inputs are finite; a program needn't handle non-finite values.
Results may differ from a plain program's by a relative error of at most 0.02.
Values may be sent and summed in bfloat16 or wider, within the bound.
No kernel may reach another device: no remote copies, remote signals or barrier semaphores. Data moves between devices by JAX's collectives and lax.ppermute only.
A program may use at most 512 MiB of HBM per device.

v0:
```python
import math
import jax
import jax.numpy as jnp
from jax import lax
from jax.sharding import PartitionSpec as P

HEADS = 32
KV_HEADS = 8
HEAD_DIM = 64
norm_eps = 1e-05
theta_log = math.log(500000.0)


def rope_tables(places, half_dim):
    freqs = jnp.exp(jnp.arange(half_dim, dtype=jnp.float32) * (-2.0 * theta_log / (2 * half_dim)))
    angles = places.astype(jnp.float32)[..., None] * freqs
    return (jnp.cos(angles), jnp.sin(angles))


def rotate(field, cos_tab, sin_tab):
    half_dim = field.shape[-1] // 2
    lower_half = field[..., :half_dim]
    upper_half = field[..., half_dim:]
    return jnp.concatenate(
        [lower_half * cos_tab - upper_half * sin_tab, upper_half * cos_tab + lower_half * sin_tab],
        -1,
    )


def unrotate(field, cos_tab, sin_tab):
    half_dim = field.shape[-1] // 2
    lower_half = field[..., :half_dim]
    upper_half = field[..., half_dim:]
    return jnp.concatenate(
        [lower_half * cos_tab + upper_half * sin_tab, upper_half * cos_tab - lower_half * sin_tab],
        -1,
    )


def times_transposed(inputs, weight):
    return lax.dot_general(
        inputs, weight, (((1,), (1,)), ((), ())), preferred_element_type=jnp.float32
    )


def rows_of(inputs, grads):
    return lax.psum_scatter(
        lax.dot_general(
            inputs, grads, (((0,), (0,)), ((), ())), preferred_element_type=jnp.float32
        ).astype(jnp.bfloat16),
        "fsdp",
        scatter_dimension=0,
        tiled=True,
    ).astype(jnp.float32)


def body(
    tokens,
    positions,
    gain_attn,
    w_query,
    w_key,
    w_value,
    w_out,
    gain_ffn,
    w_gate,
    w_up,
    w_down,
    grad_out,
):
    seq_count, tok_span, width = tokens.shape
    tok_rows = seq_count * tok_span
    seq_devs = lax.axis_size("seq")
    copies = max(KV_HEADS, seq_devs)
    repeats = copies // KV_HEADS
    q_local = HEADS // seq_devs
    kv_local = copies // seq_devs
    per_copy = HEADS // copies
    full_len = tok_span * seq_devs
    block_len = min(512, full_len)
    n_blocks = full_len // block_len
    logit_scale = HEAD_DIM ** (-0.5)
    gain_a, wq_all, wk_all, wv_all, wo_all, gain_f = (
        lax.all_gather(gain_attn, "fsdp", axis=0, tiled=True),
        lax.all_gather(w_query, "fsdp", axis=0, tiled=True),
        lax.all_gather(w_key, "fsdp", axis=0, tiled=True),
        lax.all_gather(w_value, "fsdp", axis=0, tiled=True),
        lax.all_gather(w_out, "fsdp", axis=0, tiled=True),
        lax.all_gather(gain_ffn, "fsdp", axis=0, tiled=True),
    )
    x_float = tokens.reshape(tok_rows, width).astype(jnp.float32)
    inv_one = lax.rsqrt(jnp.mean(x_float * x_float, -1, keepdims=True) + norm_eps)
    x_hat = x_float * inv_one
    gain_one = gain_a.astype(jnp.float32)
    normed_one = (x_hat * gain_one).astype(jnp.bfloat16)
    query = jnp.dot(normed_one, wq_all, preferred_element_type=jnp.float32).reshape(
        tok_rows, HEADS, HEAD_DIM
    )
    key_raw = jnp.dot(normed_one, wk_all, preferred_element_type=jnp.float32).reshape(
        tok_rows, KV_HEADS, HEAD_DIM
    )
    value_raw = jnp.dot(normed_one, wv_all, preferred_element_type=jnp.float32).reshape(
        tok_rows, KV_HEADS, HEAD_DIM
    )
    cos_tab, sin_tab = rope_tables(positions.reshape(tok_rows), HEAD_DIM // 2)
    cos_tab = cos_tab[:, None, :]
    sin_tab = sin_tab[:, None, :]
    q_rot = (
        rotate(query, cos_tab, sin_tab)
        .astype(jnp.bfloat16)
        .reshape(seq_count, tok_span, HEADS * HEAD_DIM)
    )
    k_rot = rotate(key_raw, cos_tab, sin_tab).astype(jnp.bfloat16)
    v_low = value_raw.astype(jnp.bfloat16)
    kv_pair = jnp.stack([jnp.repeat(k_rot, repeats, 1), jnp.repeat(v_low, repeats, 1)], 2)
    kv_pair = kv_pair.reshape(seq_count, tok_span, copies * 2 * HEAD_DIM)
    q_heads, kv_heads = (
        lax.all_to_all(q_rot, "seq", split_axis=2, concat_axis=1, tiled=True),
        lax.all_to_all(kv_pair, "seq", split_axis=2, concat_axis=1, tiled=True),
    )
    q_heads = q_heads.reshape(seq_count, full_len, kv_local, per_copy, HEAD_DIM)
    kv_heads = kv_heads.reshape(seq_count, full_len, kv_local, 2, HEAD_DIM)
    k_heads = kv_heads[:, :, :, 0]
    v_heads = kv_heads[:, :, :, 1]
    key_index = jnp.arange(full_len, dtype=jnp.int32)

    def block_logits(offset):
        q_block = lax.dynamic_slice_in_dim(q_heads, offset, block_len, 1)
        logits = (
            jnp.einsum("sqcgd,skcd->scgqk", q_block, k_heads, preferred_element_type=jnp.float32)
            * logit_scale
        )
        query_index = offset + jnp.arange(block_len, dtype=jnp.int32)
        allowed = key_index[None, :] <= query_index[:, None]
        return (q_block, jnp.where(allowed, logits, -1e30))

    def forward_block(block_idx, state_pair):
        attended, log_sums = state_pair
        offset = block_idx * block_len
        _, logits = block_logits(offset)
        row_max = jnp.max(logits, -1, keepdims=True)
        weights_exp = jnp.exp(logits - row_max)
        row_sum = jnp.sum(weights_exp, -1, keepdims=True)
        prob_low = (weights_exp / row_sum).astype(jnp.bfloat16)
        block_out = jnp.einsum(
            "scgqk,skcd->sqcgd", prob_low, v_heads, preferred_element_type=jnp.float32
        )
        block_out = block_out.astype(jnp.bfloat16).reshape(seq_count, block_len, q_local * HEAD_DIM)
        attended = lax.dynamic_update_slice_in_dim(attended, block_out, offset, 1)
        log_sums = lax.dynamic_update_slice_in_dim(log_sums, row_max + jnp.log(row_sum), offset, 3)
        return (attended, log_sums)

    empty_out = jnp.zeros((seq_count, full_len, q_local * HEAD_DIM), jnp.bfloat16)
    empty_lse = jnp.zeros((seq_count, kv_local, per_copy, full_len, 1), jnp.float32)
    attended, log_sums = lax.fori_loop(0, n_blocks, forward_block, (empty_out, empty_lse))
    o_tokens = lax.all_to_all(attended, "seq", split_axis=1, concat_axis=2, tiled=True).reshape(
        tok_rows, HEADS * HEAD_DIM
    )
    resid = x_float + jnp.dot(o_tokens, wo_all, preferred_element_type=jnp.float32)
    inv_two = lax.rsqrt(jnp.mean(resid * resid, -1, keepdims=True) + norm_eps)
    resid_hat = resid * inv_two
    gain_two = gain_f.astype(jnp.float32)
    normed_two = (resid_hat * gain_two).astype(jnp.bfloat16)
    pieces = (
        lax.all_gather(w_gate, "fsdp", axis=0, tiled=True),
        lax.all_gather(w_up, "fsdp", axis=0, tiled=True),
    )
    columns = normed_two
    gate = jnp.dot(columns, pieces[0], preferred_element_type=jnp.float32)
    upper = jnp.dot(columns, pieces[1], preferred_element_type=jnp.float32)
    gate_sig = jax.nn.sigmoid(gate)
    gate_act = gate * gate_sig
    hidden = (gate_act * upper).astype(jnp.bfloat16)
    columns = hidden
    branch_out = jnp.dot(
        columns,
        lax.all_gather(w_down, "fsdp", axis=0, tiled=True),
        preferred_element_type=jnp.float32,
    )
    layer_out = (resid + branch_out).astype(jnp.bfloat16).reshape(seq_count, tok_span, width)
    cot_rows = grad_out.reshape(tok_rows, width)
    grad_down = rows_of(hidden, cot_rows)
    d_hidden = times_transposed(cot_rows, lax.all_gather(w_down, "fsdp", axis=0, tiled=True))
    d_gate = (d_hidden * upper * (gate_sig + gate_act * (1.0 - gate_sig))).astype(jnp.bfloat16)
    d_up = (d_hidden * gate_act).astype(jnp.bfloat16)
    grad_gate = rows_of(normed_two, d_gate)
    grad_upper = rows_of(normed_two, d_up)
    pieces = lax.all_gather((w_gate, w_up), "fsdp", axis=0, tiled=True)
    d_normed_two = times_transposed(d_gate, pieces[0]) + times_transposed(d_up, pieces[1])
    d_hat_two = d_normed_two * gain_two
    grad_gain_two = jnp.sum(d_normed_two * resid_hat, 0)
    d_resid = cot_rows.astype(jnp.float32) + inv_two * (
        d_hat_two - resid_hat * jnp.mean(d_hat_two * resid_hat, -1, keepdims=True)
    )
    d_branch = d_resid.astype(jnp.bfloat16)
    grad_out_w = lax.dot_general(
        o_tokens, d_branch, (((0,), (0,)), ((), ())), preferred_element_type=jnp.float32
    )
    d_attended = (
        times_transposed(d_branch, wo_all)
        .astype(jnp.bfloat16)
        .reshape(seq_count, tok_span, HEADS * HEAD_DIM)
    )
    d_heads = lax.all_to_all(d_attended, "seq", split_axis=2, concat_axis=1, tiled=True)
    d_heads = d_heads.reshape(seq_count, full_len, kv_local, per_copy, HEAD_DIM)

    def backward_block(block_idx, state_three):
        d_query_h, d_key_h, d_value_h = state_three
        offset = block_idx * block_len
        q_block, logits = block_logits(offset)
        probs = jnp.exp(logits - lax.dynamic_slice_in_dim(log_sums, offset, block_len, 3))
        prob_low = probs.astype(jnp.bfloat16)
        grad_block = lax.dynamic_slice_in_dim(d_heads, offset, block_len, 1)
        d_probs = jnp.einsum(
            "sqcgd,skcd->scgqk", grad_block, v_heads, preferred_element_type=jnp.float32
        )
        inner = jnp.sum(probs * d_probs, -1, keepdims=True)
        d_logits = (probs * (d_probs - inner)).astype(jnp.bfloat16)
        dq_block = (
            jnp.einsum("scgqk,skcd->sqcgd", d_logits, k_heads, preferred_element_type=jnp.float32)
            * logit_scale
        )
        d_key_h = (
            d_key_h
            + jnp.einsum("scgqk,sqcgd->skcd", d_logits, q_block, preferred_element_type=jnp.float32)
            * logit_scale
        )
        d_value_h = d_value_h + jnp.einsum(
            "scgqk,sqcgd->skcd", prob_low, grad_block, preferred_element_type=jnp.float32
        )
        d_query_h = lax.dynamic_update_slice_in_dim(
            d_query_h, dq_block.astype(jnp.bfloat16), offset, 1
        )
        return (d_query_h, d_key_h, d_value_h)

    empty_dq = jnp.zeros((seq_count, full_len, kv_local, per_copy, HEAD_DIM), jnp.bfloat16)
    empty_dkv = jnp.zeros((seq_count, full_len, kv_local, HEAD_DIM), jnp.float32)
    d_query_h, d_key_h, d_value_h = lax.fori_loop(
        0, n_blocks, backward_block, (empty_dq, empty_dkv, empty_dkv)
    )
    d_kv_pair = (
        jnp.stack([d_key_h, d_value_h], 3)
        .astype(jnp.bfloat16)
        .reshape(seq_count, full_len, kv_local * 2 * HEAD_DIM)
    )
    d_q_pack = d_query_h.reshape(seq_count, full_len, q_local * HEAD_DIM)
    dq_tokens, dkv_tokens = (
        lax.all_to_all(d_q_pack, "seq", split_axis=1, concat_axis=2, tiled=True),
        lax.all_to_all(d_kv_pair, "seq", split_axis=1, concat_axis=2, tiled=True),
    )
    dq_rot = dq_tokens.reshape(tok_rows, HEADS, HEAD_DIM).astype(jnp.float32)
    dkv_sum = jnp.sum(
        dkv_tokens.reshape(tok_rows, KV_HEADS, repeats, 2, HEAD_DIM).astype(jnp.float32), 2
    )
    d_query = (
        unrotate(dq_rot, cos_tab, sin_tab).astype(jnp.bfloat16).reshape(tok_rows, HEADS * HEAD_DIM)
    )
    d_key = (
        unrotate(dkv_sum[:, :, 0], cos_tab, sin_tab)
        .astype(jnp.bfloat16)
        .reshape(tok_rows, KV_HEADS * HEAD_DIM)
    )
    d_value = dkv_sum[:, :, 1].astype(jnp.bfloat16).reshape(tok_rows, KV_HEADS * HEAD_DIM)
    d_qkv = jnp.concatenate([d_query, d_key, d_value], 1)
    grad_qkv = lax.dot_general(
        normed_one, d_qkv, (((0,), (0,)), ((), ())), preferred_element_type=jnp.float32
    )
    q_width = HEADS * HEAD_DIM
    kv_width = KV_HEADS * HEAD_DIM
    grad_query = grad_qkv[:, :q_width]
    grad_key = grad_qkv[:, q_width : q_width + kv_width]
    grad_value = grad_qkv[:, q_width + kv_width :]
    d_normed_one = (
        times_transposed(d_query, wq_all)
        + times_transposed(d_key, wk_all)
        + times_transposed(d_value, wv_all)
    )
    d_hat_one = d_normed_one * gain_one
    grad_gain_one = jnp.sum(d_normed_one * x_hat, 0)
    d_input = d_resid + inv_one * (
        d_hat_one - x_hat * jnp.mean(d_hat_one * x_hat, -1, keepdims=True)
    )
    grad_tokens = d_input.astype(jnp.bfloat16).reshape(seq_count, tok_span, width)
    sum_q, sum_k, sum_v, sum_o, sum_g1, sum_g2 = (
        lax.psum_scatter(
            grad_query.astype(jnp.bfloat16), "fsdp", scatter_dimension=0, tiled=True
        ).astype(jnp.float32),
        lax.psum_scatter(
            grad_key.astype(jnp.bfloat16), "fsdp", scatter_dimension=0, tiled=True
        ).astype(jnp.float32),
        lax.psum_scatter(
            grad_value.astype(jnp.bfloat16), "fsdp", scatter_dimension=0, tiled=True
        ).astype(jnp.float32),
        lax.psum_scatter(
            grad_out_w.astype(jnp.bfloat16), "fsdp", scatter_dimension=0, tiled=True
        ).astype(jnp.float32),
        lax.psum_scatter(
            grad_gain_one.astype(jnp.bfloat16), "fsdp", scatter_dimension=0, tiled=True
        ).astype(jnp.float32),
        lax.psum_scatter(
            grad_gain_two.astype(jnp.bfloat16), "fsdp", scatter_dimension=0, tiled=True
        ).astype(jnp.float32),
    )
    all_q, all_k, all_v, all_o, all_g1, all_g2, all_gate, all_up, all_down = (
        lax.psum(sum_q.astype(jnp.bfloat16), "seq").astype(jnp.float32),
        lax.psum(sum_k.astype(jnp.bfloat16), "seq").astype(jnp.float32),
        lax.psum(sum_v.astype(jnp.bfloat16), "seq").astype(jnp.float32),
        lax.psum(sum_o.astype(jnp.bfloat16), "seq").astype(jnp.float32),
        lax.psum(sum_g1.astype(jnp.bfloat16), "seq").astype(jnp.float32),
        lax.psum(sum_g2.astype(jnp.bfloat16), "seq").astype(jnp.float32),
        lax.psum(grad_gate.astype(jnp.bfloat16), "seq").astype(jnp.float32),
        lax.psum(grad_upper.astype(jnp.bfloat16), "seq").astype(jnp.float32),
        lax.psum(grad_down.astype(jnp.bfloat16), "seq").astype(jnp.float32),
    )
    return (
        layer_out,
        grad_tokens,
        all_g1,
        all_q,
        all_k,
        all_v,
        all_o,
        all_g2,
        all_gate,
        all_up,
        all_down,
    )


def solution(mesh):
    placed = (
        P("fsdp", "seq", None),
        P("fsdp", "seq"),
        P("fsdp"),
        P("fsdp", None),
        P("fsdp", None),
        P("fsdp", None),
        P("fsdp", None),
        P("fsdp"),
        P("fsdp", None),
        P("fsdp", None),
        P("fsdp", None),
        P("fsdp", "seq", None),
    )
    return jax.shard_map(
        body,
        mesh=mesh,
        in_specs=placed,
        out_specs=(
            P("fsdp", "seq", None),
            P("fsdp", "seq", None),
            P("fsdp"),
            P("fsdp", None),
            P("fsdp", None),
            P("fsdp", None),
            P("fsdp", None),
            P("fsdp"),
            P("fsdp", None),
            P("fsdp", None),
            P("fsdp", None),
        ),
        check_vma=False,
    )
```

profile of v0, /device:TPU:0, one launch (start us, length us, event | category | flops | bytes accessed | tf_op | source)
XLA Modules:
  0.0 3219.5 jit_solution(10981159727728233364)
XLA Ops:
  22.9 25.0 all-gather.14.cloned.1.call-done
  50.9 34.2 %all-gather.12.cloned.1.call-done = bf16[2048,512]{1,0:T(8,128)(2,1)} async-done(((bf16[512,512]{1,0:T(8,128)(2,1)}), bf16[2048,512]{1,0:T(8,128)(2,1)}) %all-gather.12.cloned.1.call-update) | async-done | bytes 2097168 | tf_op jit(solution)/shard_map/all_gather | solution.py:86
  97.8 76.8 %all-gather.10.cloned.1.call-done = bf16[2048,2048]{1,0:T(8,128)(2,1)} async-done(((bf16[512,2048]{1,0:T(8,128)(2,1)}), bf16[2048,2048]{1,0:T(8,128)(2,1)}) %all-gather.10.cloned.1.call-update) | async-done | bytes 8388624 | tf_op jit(solution)/shard_map/all_gather | solution.py:85
  200.2 25.9 all-to-all-done
  229.3 30.2 while.34
  272.3 18.4 all-to-all-done.2
  299.4 263.4 %all-gather.18.cloned.1.call-done = bf16[2048,8192]{1,0:T(8,128)(2,1)} async-done(((bf16[512,8192]{1,0:T(8,128)(2,1)}), bf16[2048,8192]{1,0:T(8,128)(2,1)}) %all-gather.18.cloned.1.call-update) | async-done | bytes 33554448 | tf_op jit(solution)/shard_map/all_gather | solution.py:165
  562.9 21.9 fusion.80
  584.8 277.0 %all-gather.20.cloned.1.call-done = bf16[2048,8192]{1,0:T(8,128)(2,1)} async-done(((bf16[512,8192]{1,0:T(8,128)(2,1)}), bf16[2048,8192]{1,0:T(8,128)(2,1)}) %all-gather.20.cloned.1.call-update) | async-done | bytes 33554448 | tf_op jit(solution)/shard_map/all_gather | solution.py:166
  861.8 21.2 fusion.81
  883.1 277.8 %all-gather.22.cloned.1.call-done = bf16[8192,2048]{1,0:T(8,128)(2,1)} async-done(((bf16[2048,2048]{1,0:T(8,128)(2,1)}), bf16[8192,2048]{1,0:T(8,128)(2,1)}) %all-gather.22.cloned.1.call-update) | async-done | bytes 33554448 | tf_op jit(solution)/shard_map/all_gather | solution.py:177
  1160.9 23.0 multiply_convert_fusion
  1183.9 17.5 fusion.82
  1201.3 18.7 multiply_reduce_fusion
  1235.6 26.6 all-to-all-done.3
  1265.2 98.1 %while.35 = (s32[]{:T(128)}, bf16[2,1024,1,4,64]{1,4,3,0,2:T(8,128)(2,1)}, f32[2,1024,1,64]{1,3,0,2:T(8,128)}, f32[2,1024,1,64]{1,3,0,2:T(8,128)}, bf16[2,1024,1...) while((s32[]{:T(128)}, ...), condition=%wide.region_9.10_spmd.clone, body=%wide.region_7.0_spmd.clone.sunk | while | flops 2748969472 | bytes 213307824 | solution.py:238
  1391.8 23.2 all-to-all-done.4
  1515.6 89.9 %reduce-scatter.20.cloned.1.call-done = bf16[512,2048]{1,0:T(8,128)(2,1)} async-done(((bf16[2048,2048]{1,0:T(8,128)(2,1)}), bf16[512,2048]{1,0:T(8,128)(2,1)}) %reduce-scatter.20.cloned.1.call-update) | async-done | bytes 2097168 | tf_op jit(solution)/shard_map/reduce_scatter | solution.py:294
  1605.5 90.4 %reduce-scatter.14.cloned.1.call-done = bf16[512,2048]{1,0:T(8,128)(2,1)} async-done(((bf16[2048,2048]{1,0:T(8,128)(2,1)}), bf16[512,2048]{1,0:T(8,128)(2,1)}) %reduce-scatter.14.cloned.1.call-update) | async-done | bytes 2097168 | tf_op jit(solution)/shard_map/reduce_scatter | solution.py:285
  1695.9 291.6 %reduce-scatter.22.cloned.1.call-done = bf16[512,8192]{1,0:T(8,128)(2,1)} async-done(((bf16[2048,8192]{1,0:T(8,128)(2,1)}), bf16[512,8192]{1,0:T(8,128)(2,1)}) %reduce-scatter.22.cloned.1.call-update) | async-done | bytes 8388624
  1987.5 292.0 %reduce-scatter.24.cloned.1.call-done = bf16[512,8192]{1,0:T(8,128)(2,1)} async-done(((bf16[2048,8192]{1,0:T(8,128)(2,1)}), bf16[512,8192]{1,0:T(8,128)(2,1)}) %reduce-scatter.24.cloned.1.call-update) | async-done | bytes 8388624
  2279.6 291.6 %reduce-scatter.26.cloned.1.call-done = bf16[2048,2048]{1,0:T(8,128)(2,1)} async-done(((bf16[8192,2048]{1,0:T(8,128)(2,1)}), bf16[2048,2048]{1,0:T(8,128)(2,1)}) %reduce-scatter.26.cloned.1.call-update) | async-done | bytes 8388624
  2573.0 19.2 fusion.62
  2621.5 547.0 %all-reduce.10.cloned.1.call-done = (bf16[512,2048]{1,0:T(8,128)(2,1)}, bf16[512,512]{1,0:T(8,128)(2,1)}, bf16[512,512]{1,0:T(8,128)(2,1)}, bf16[512,2048]{1,0:T...) async-done(((bf16[512,2048]{1,0:T(8,128)(2,1)}, bf16[512,512]{1,0:T(8,128)(2,1)}, bf16[512,512]{1,0:T(8,128)(2,1)}, ...) | async-done | bytes 30408720 | tf_op jit(solution)/shard_map/psum | solution.py:305
  (248 shorter events, 431.2 us)
Async XLA Ops:
  7.2 40.7 %all-gather.14.cloned.1.call-start = ((), (), s32[]{:S(2)}) async-start(), calls=%async_computation.15 | async-start | bytes 2621440 | tf_op jit(solution)/shard_map/all_gather | solution.py:87
  7.9 77.2 %all-gather.12.cloned.1.call-start = ((), (), s32[]{:S(2)}) async-start(), calls=%async_computation.14 | async-start | bytes 2621440 | tf_op jit(solution)/shard_map/all_gather | solution.py:86
  8.7 165.9 %all-gather.10.cloned.1.call-start = ((), (), s32[]{:S(2)}) async-start(), calls=%async_computation.13 | async-start | bytes 10485760 | tf_op jit(solution)/shard_map/all_gather | solution.py:85
  9.4 282.2 %all-gather.16.cloned.1.call-start = ((), (), s32[]{:S(2)}) async-start(), calls=%async_computation.16 | async-start | bytes 10485760 | tf_op jit(solution)/shard_map/all_gather | solution.py:88
  10.0 552.9 %all-gather.18.cloned.1.call-start = ((), (), s32[]{:S(2)}) async-start(), calls=%async_computation.17 | async-start | bytes 41943040 | tf_op jit(solution)/shard_map/all_gather | solution.py:165
  10.6 851.3 %all-gather.20.cloned.1.call-start = ((), (), s32[]{:S(2)}) async-start(), calls=%async_computation.18 | async-start | bytes 41943040 | tf_op jit(solution)/shard_map/all_gather | solution.py:166
  11.2 1149.7 %all-gather.22.cloned.1.call-start = ((), (), s32[]{:S(2)}) async-start(), calls=%async_computation.19 | async-start | bytes 41943040 | tf_op jit(solution)/shard_map/all_gather | solution.py:177
  22.6 170.5 %copy-start.20 = (f32[256,32]{0,1:T(8,128)}, f32[256,32]{0,1:T(8,128)S(1)}, u32[]{:S(2)}) copy-start(f32[256,32]{0,1:T(8,128)S(1)} %get-tuple-element.425) | copy-start | bytes 98308
  93.2 101.4 %all-to-all-start.1 = ((bf16[2,128,1024]{1,0,2:T(2,128)(2,1)}), bf16[2,128,1024]{1,0,2:T(2,128)(2,1)S(1)}, u32[]{:S(2)}, u32[]{:S(2)}) async-start(bf16[2,128,1024]{1,0,2:T(2,128)(2,1)} %reshape.420), calls=%async_computation.1 | async-start | bytes 1048576 | tf_op jit(solution)/shard_map/all_to_all | solution.py:119
  194.6 31.5 all-to-all-start
  260.5 30.2 all-to-all-start.2
  299.4 562.4 %copy-start.9 = (bf16[256,2048]{1,0:T(8,128)(2,1)}, bf16[256,2048]{1,0:T(8,128)(2,1)S(1)}, u32[]{:S(2)}) copy-start(bf16[256,2048]{1,0:T(8,128)(2,1)S(1)} %multiply_convert_fusion.4) | copy-start | bytes 3145732
  584.8 576.1 %copy-start.15 = (bf16[2,128,2048]{2,1,0:T(8,128)(2,1)S(1)}, bf16[2,128,2048]{2,1,0:T(8,128)(2,1)}, u32[]{:S(2)}) copy-start(bf16[2,128,2048]{2,1,0:T(8,128)(2,1)} %param.27) | copy-start | bytes 3145732
  1231.0 31.2 all-to-all-start.3
  1366.0 18.9 all-to-all-start.5
  1384.9 30.1 all-to-all-start.4
  1388.5 123.1 %reduce-scatter.16.cloned.1.call-start = ((), (), s32[]{:S(2)}) async-start(), calls=%async_computation.21 | async-start | bytes 2621440 | tf_op jit(solution)/shard_map/reduce_scatter | solution.py:288
  1443.9 71.7 %reduce-scatter.18.cloned.1.call-start = ((), (), s32[]{:S(2)}) async-start(), calls=%async_computation.22 | async-start | bytes 2621440 | tf_op jit(solution)/shard_map/reduce_scatter | solution.py:291
  1444.6 160.9 %reduce-scatter.20.cloned.1.call-start = ((), (), s32[]{:S(2)}) async-start(), calls=%async_computation.23 | async-start | bytes 10485760 | tf_op jit(solution)/shard_map/reduce_scatter | solution.py:294
  1452.5 243.4 %reduce-scatter.14.cloned.1.call-start = ((), (), s32[]{:S(2)}) async-start(), calls=%async_computation.20 | async-start | bytes 10485760 | tf_op jit(solution)/shard_map/reduce_scatter | solution.py:285
  1461.3 526.2 %reduce-scatter.22.cloned.1.call-start = ((), (), s32[]{:S(2)}) async-start(), calls=%async_computation.24 | async-start | bytes 41943040
  1477.9 801.6 %reduce-scatter.24.cloned.1.call-start = ((), (), s32[]{:S(2)}) async-start(), calls=%async_computation.25 | async-start | bytes 41943040
  1494.9 1076.2 %reduce-scatter.26.cloned.1.call-start = ((), (), s32[]{:S(2)}) async-start(), calls=%async_computation.26 | async-start | bytes 41943040
  1511.5 1657.0 %all-reduce.10.cloned.1.call-start = ((), (), s32[]{:S(2)}) async-start(), calls=%async_computation.27 | async-start | bytes 60817408 | tf_op jit(solution)/shard_map/psum | solution.py:305
  (40 other events, 515.6 us)
Sparse Core Ops, SparseCore 0:
  9.9 38.0 all-gather.13
  49.8 35.2 all-gather.11
  87.0 87.5 all-gather.9
  176.3 87.5 all-gather.15
  265.6 297.2 all-gather.17
  564.6 297.2 all-gather.19
  863.6 297.2 all-gather.21
  1444.0 33.0 reduce-scatter.15
  1480.4 35.1 reduce-scatter.17
  1519.1 86.3 reduce-scatter.19
  1609.5 86.4 reduce-scatter.13
  1698.8 288.6 reduce-scatter.21
  1990.9 288.6 reduce-scatter.23
  2282.5 288.6 reduce-scatter.25
  2574.8 593.6 all-reduce.9
where the time goes:
time: 3230 us; the launch traced here: 3220 us
  waiting for transfers between devices  2670 us (83%)
  matrix products  305 us (9%)
  other arithmetic  88.7 us (3%)
  local copies, waits for them, and re-layouts  69.2 us (2%)
  blocking collectives  42.4 us (1%)
    unnamed x18, waiting for transfers between devices  880 us
    psum x1, waiting for transfers between devices, body(): lax.psum(sum_q.astype(jnp.bfloat16), 'seq').astype(jnp.float32)  547 us
    all_gather x1, waiting for transfers between devices, body(): lax.all_gather(w_down, 'fsdp', axis=0, tiled=True)  278 us
    all_gather x1, waiting for transfers between devices, body(): lax.all_gather(w_up, 'fsdp', axis=0, tiled=True)  277 us
    all_gather x1, waiting for transfers between devices, body(): lax.all_gather(w_gate, 'fsdp', axis=0, tiled=True)  263 us
    reduce_scatter x1, waiting for transfers between devices, body(): lax.psum_scatter(grad_query.astype(jnp.bfloat16), 'fsdp', scatter_dimensi...  90.4 us
    reduce_scatter x1, waiting for transfers between devices, body(): lax.psum_scatter(grad_out_w.astype(jnp.bfloat16), 'fsdp', scatter_dimensi...  89.9 us
    all_gather x1, waiting for transfers between devices, body(): lax.all_gather(w_query, 'fsdp', axis=0, tiled=True)  76.8 us
  transfers between devices with their start and end apart: 21, of which 18 were waited for; matrix products, arithmetic and copies ran while one was open for 7% of the time, Pallas kernels for 0%

commit v1 on v0

--- a/solution.py
+++ b/solution.py
@@ -302,7 +302,7 @@
         ).astype(jnp.float32),
     )
     all_q, all_k, all_v, all_o, all_g1, all_g2, all_gate, all_up, all_down = (
-        lax.psum(sum_q.astype(jnp.bfloat16), "seq").astype(jnp.float32),
+        jnp.sum(lax.all_gather(sum_q.astype(jnp.bfloat16), "seq"), axis=0).astype(jnp.float32),
         lax.psum(sum_k.astype(jnp.bfloat16), "seq").astype(jnp.float32),
         lax.psum(sum_v.astype(jnp.bfloat16), "seq").astype(jnp.float32),
         lax.psum(sum_o.astype(jnp.bfloat16), "seq").astype(jnp.float32),

time: 3230 us -> 3340 us (1.034)
  waiting for transfers between devices: 2670 us -> 2770 us
    all_gather x0 -> x1, waiting for transfers between devices: none -> 101 us  [body(): lax.all_gather(sum_q.astype(jnp.bfloat16), 'seq')]
    reduce_scatter x1, waiting for transfers between devices: 90.4 us -> 19.7 us  [body(): lax.psum_scatter(grad_query.astype(jnp.bfloat16), 'fsdp', scatter_dimensi...]
    reduce_scatter x1, waiting for transfers between devices: 0.02 us -> 38.4 us  [body(): lax.psum_scatter(grad_key.astype(jnp.bfloat16), 'fsdp', scatter_dimension...]
    reduce_scatter x1, waiting for transfers between devices: 4.03 us -> 38 us  [body(): lax.psum_scatter(grad_value.astype(jnp.bfloat16), 'fsdp', scatter_dimensi...]
    unnamed x18 -> x19, waiting for transfers between devices: 880 us -> 880 us
  transfers between devices with their start and end apart: 21 -> 22, of which waited for: 18 -> 20; matrix products, arithmetic and copies ran while one was open for 7% -> 7% of each run, Pallas kernels for 0% -> 0%
where the time goes in v1:
time: 3340 us; the launch traced here: 3330 us
  waiting for transfers between devices  2770 us (83%)
  matrix products  308 us (9%)
  other arithmetic  99.6 us (3%)
  local copies, waits for them, and re-layouts  69.2 us (2%)
  blocking collectives  42.4 us (1%)
    unnamed x19, waiting for transfers between devices  880 us
    psum x1, waiting for transfers between devices, body(): lax.psum(sum_k.astype(jnp.bfloat16), 'seq').astype(jnp.float32)  542 us
    all_gather x1, waiting for transfers between devices, body(): lax.all_gather(w_down, 'fsdp', axis=0, tiled=True)  278 us
    all_gather x1, waiting for transfers between devices, body(): lax.all_gather(w_up, 'fsdp', axis=0, tiled=True)  277 us
    all_gather x1, waiting for transfers between devices, body(): lax.all_gather(w_gate, 'fsdp', axis=0, tiled=True)  263 us
    all_gather x1, waiting for transfers between devices, body(): lax.all_gather(sum_q.astype(jnp.bfloat16), 'seq')  101 us
    reduce_scatter x1, waiting for transfers between devices, body(): lax.psum_scatter(grad_out_w.astype(jnp.bfloat16), 'fsdp', scatter_dimensi...  90.4 us
    all_gather x1, waiting for transfers between devices, body(): lax.all_gather(w_query, 'fsdp', axis=0, tiled=True)  76.8 us
  transfers between devices with their start and end apart: 22, of which 20 were waited for; matrix products, arithmetic and copies ran while one was open for 7% of the time, Pallas kernels for 0%

profile of v1, /device:TPU:0, one launch (start us, length us, event | category | flops | bytes accessed | tf_op | source)
XLA Modules:
  0.0 3331.4 jit_solution(6209017977008992249)
XLA Ops:
  22.9 25.0 all-gather.16.cloned.1.call-done
  50.9 34.2 %all-gather.14.cloned.1.call-done = bf16[2048,512]{1,0:T(8,128)(2,1)} async-done(((bf16[512,512]{1,0:T(8,128)(2,1)}), bf16[2048,512]{1,0:T(8,128)(2,1)}) %all-gather.14.cloned.1.call-update) | async-done | bytes 2097168 | tf_op jit(solution)/shard_map/all_gather | solution.py:86
  97.8 76.8 %all-gather.12.cloned.1.call-done = bf16[2048,2048]{1,0:T(8,128)(2,1)} async-done(((bf16[512,2048]{1,0:T(8,128)(2,1)}), bf16[2048,2048]{1,0:T(8,128)(2,1)}) %all-gather.12.cloned.1.call-update) | async-done | bytes 8388624 | tf_op jit(solution)/shard_map/all_gather | solution.py:85
  200.2 25.9 all-to-all-done
  229.3 30.3 while.34
  299.5 263.4 %all-gather.20.cloned.1.call-done = bf16[2048,8192]{1,0:T(8,128)(2,1)} async-done(((bf16[512,8192]{1,0:T(8,128)(2,1)}), bf16[2048,8192]{1,0:T(8,128)(2,1)}) %all-gather.20.cloned.1.call-update) | async-done | bytes 33554448 | tf_op jit(solution)/shard_map/all_gather | solution.py:165
  562.9 21.9 fusion.80
  584.8 277.0 %all-gather.22.cloned.1.call-done = bf16[2048,8192]{1,0:T(8,128)(2,1)} async-done(((bf16[512,8192]{1,0:T(8,128)(2,1)}), bf16[2048,8192]{1,0:T(8,128)(2,1)}) %all-gather.22.cloned.1.call-update) | async-done | bytes 33554448 | tf_op jit(solution)/shard_map/all_gather | solution.py:166
  861.8 21.2 fusion.81
  883.1 277.8 %all-gather.24.cloned.1.call-done = bf16[8192,2048]{1,0:T(8,128)(2,1)} async-done(((bf16[2048,2048]{1,0:T(8,128)(2,1)}), bf16[8192,2048]{1,0:T(8,128)(2,1)}) %all-gather.24.cloned.1.call-update) | async-done | bytes 33554448 | tf_op jit(solution)/shard_map/all_gather | solution.py:177
  1160.9 22.9 multiply_convert_fusion
  1235.6 26.6 all-to-all-done.3
  1265.2 98.2 %while.35 = (s32[]{:T(128)}, bf16[2,1024,1,4,64]{1,4,3,0,2:T(8,128)(2,1)}, f32[2,1024,1,64]{1,3,0,2:T(8,128)}, f32[2,1024,1,64]{1,3,0,2:T(8,128)}, bf16[2,1024,1...) while((s32[]{:T(128)}, ...), condition=%wide.region_9.10_spmd.clone, body=%wide.region_7.0_spmd.clone.sunk | while | flops 2748969472 | bytes 213307824 | solution.py:238
  1391.9 23.2 all-to-all-done.4
  1512.7 19.7 reduce-scatter.14.cloned.1.call-done
  1532.5 38.4 %reduce-scatter.16.cloned.1.call-done = bf16[512,512]{1,0:T(8,128)(2,1)} async-done(((bf16[2048,512]{1,0:T(8,128)(2,1)}), bf16[512,512]{1,0:T(8,128)(2,1)}) %reduce-scatter.16.cloned.1.call-update) | async-done | bytes 524304 | tf_op jit(solution)/shard_map/reduce_scatter | solution.py:288
  1570.9 38.0 %reduce-scatter.18.cloned.1.call-done = bf16[512,512]{1,0:T(8,128)(2,1)} async-done(((bf16[2048,512]{1,0:T(8,128)(2,1)}), bf16[512,512]{1,0:T(8,128)(2,1)}) %reduce-scatter.18.cloned.1.call-update) | async-done | bytes 524304 | tf_op jit(solution)/shard_map/reduce_scatter | solution.py:291
  1608.9 90.4 %reduce-scatter.20.cloned.1.call-done = bf16[512,2048]{1,0:T(8,128)(2,1)} async-done(((bf16[2048,2048]{1,0:T(8,128)(2,1)}), bf16[512,2048]{1,0:T(8,128)(2,1)}) %reduce-scatter.20.cloned.1.call-update) | async-done | bytes 2097168 | tf_op jit(solution)/shard_map/reduce_scatter | solution.py:294
  1699.3 291.6 %reduce-scatter.22.cloned.1.call-done = bf16[512,8192]{1,0:T(8,128)(2,1)} async-done(((bf16[2048,8192]{1,0:T(8,128)(2,1)}), bf16[512,8192]{1,0:T(8,128)(2,1)}) %reduce-scatter.22.cloned.1.call-update) | async-done | bytes 8388624
  1990.9 292.0 %reduce-scatter.24.cloned.1.call-done = bf16[512,8192]{1,0:T(8,128)(2,1)} async-done(((bf16[2048,8192]{1,0:T(8,128)(2,1)}), bf16[512,8192]{1,0:T(8,128)(2,1)}) %reduce-scatter.24.cloned.1.call-update) | async-done | bytes 8388624
  2282.9 291.6 %reduce-scatter.26.cloned.1.call-done = bf16[2048,2048]{1,0:T(8,128)(2,1)} async-done(((bf16[8192,2048]{1,0:T(8,128)(2,1)}), bf16[2048,2048]{1,0:T(8,128)(2,1)}) %reduce-scatter.26.cloned.1.call-update) | async-done | bytes 8388624
  2576.4 20.5 fusion.62
  2626.2 101.3 %all-gather.26.cloned.1.call-done = bf16[4096,2048]{1,0:T(8,128)(2,1)} async-done(((bf16[512,2048]{1,0:T(8,128)(2,1)}), bf16[4096,2048]{1,0:T(8,128)(2,1)}) %all-gather.26.cloned.1.call-update) | async-done | bytes 16777232 | tf_op jit(solution)/shard_map/all_gather | solution.py:305
  2740.4 542.1 %all-reduce.10.cloned.1.call-done = (bf16[512,512]{1,0:T(8,128)(2,1)}, bf16[512,512]{1,0:T(8,128)(2,1)}, bf16[512,2048]{1,0:T(8,128)(2,1)}, bf16[512,8192]{1,0:T...) async-done(((bf16[512,512]{1,0:T(8,128)(2,1)}, bf16[512,512]{1,0:T(8,128)(2,1)}, bf16[512,2048]{1,0:T(8,128)(2,1)}, bf16[512,8192]{1,0:T(8,128)(2,1)}, ...) | async-done | bytes 28311568 | tf_op jit(solution)/shard_map/psum | solution.py:306
  (248 shorter events, 493.8 us)
Async XLA Ops:
  7.2 40.7 %all-gather.16.cloned.1.call-start = ((), (), s32[]{:S(2)}) async-start(), calls=%async_computation.15 | async-start | bytes 2621440 | tf_op jit(solution)/shard_map/all_gather | solution.py:87
  7.9 77.2 %all-gather.14.cloned.1.call-start = ((), (), s32[]{:S(2)}) async-start(), calls=%async_computation.14 | async-start | bytes 2621440 | tf_op jit(solution)/shard_map/all_gather | solution.py:86
  8.7 165.9 %all-gather.12.cloned.1.call-start = ((), (), s32[]{:S(2)}) async-start(), calls=%async_computation.13 | async-start | bytes 10485760 | tf_op jit(solution)/shard_map/all_gather | solution.py:85
  9.4 282.3 %all-gather.18.cloned.1.call-start = ((), (), s32[]{:S(2)}) async-start(), calls=%async_computation.16 | async-start | bytes 10485760 | tf_op jit(solution)/shard_map/all_gather | solution.py:88
  10.0 552.9 %all-gather.20.cloned.1.call-start = ((), (), s32[]{:S(2)}) async-start(), calls=%async_computation.17 | async-start | bytes 41943040 | tf_op jit(solution)/shard_map/all_gather | solution.py:165
  10.6 851.3 %all-gather.22.cloned.1.call-start = ((), (), s32[]{:S(2)}) async-start(), calls=%async_computation.18 | async-start | bytes 41943040 | tf_op jit(solution)/shard_map/all_gather | solution.py:166
  11.2 1149.7 %all-gather.24.cloned.1.call-start = ((), (), s32[]{:S(2)}) async-start(), calls=%async_computation.19 | async-start | bytes 41943040 | tf_op jit(solution)/shard_map/all_gather | solution.py:177
  93.2 101.4 %all-to-all-start.1 = ((bf16[2,128,1024]{1,0,2:T(2,128)(2,1)}), bf16[2,128,1024]{1,0,2:T(2,128)(2,1)S(1)}, u32[]{:S(2)}, u32[]{:S(2)}) async-start(bf16[2,128,1024]{1,0,2:T(2,128)(2,1)} %reshape.420), calls=%async_computation.1 | async-start | bytes 1048576 | tf_op jit(solution)/shard_map/all_to_all | solution.py:119
  194.6 31.5 all-to-all-start
  260.5 30.2 all-to-all-start.2
  299.5 562.4 %copy-start.9 = (bf16[256,2048]{1,0:T(8,128)(2,1)}, bf16[256,2048]{1,0:T(8,128)(2,1)S(1)}, u32[]{:S(2)}) copy-start(bf16[256,2048]{1,0:T(8,128)(2,1)S(1)} %multiply_convert_fusion.4) | copy-start | bytes 3145732
  584.8 576.1 %copy-start.15 = (bf16[2,128,2048]{2,1,0:T(8,128)(2,1)S(1)}, bf16[2,128,2048]{2,1,0:T(8,128)(2,1)}, u32[]{:S(2)}) copy-start(bf16[2,128,2048]{2,1,0:T(8,128)(2,1)} %param.27) | copy-start | bytes 3145732
  1230.9 31.2 all-to-all-start.3
  1366.1 18.9 all-to-all-start.5
  1385.0 30.1 all-to-all-start.4
  1388.5 143.9 %reduce-scatter.14.cloned.1.call-start = ((), (), s32[]{:S(2)}) async-start(), calls=%async_computation.20 | async-start | bytes 10485760 | tf_op jit(solution)/shard_map/reduce_scatter | solution.py:285
  1447.9 123.0 %reduce-scatter.16.cloned.1.call-start = ((), (), s32[]{:S(2)}) async-start(), calls=%async_computation.21 | async-start | bytes 2621440 | tf_op jit(solution)/shard_map/reduce_scatter | solution.py:288
  1452.5 156.4 %reduce-scatter.18.cloned.1.call-start = ((), (), s32[]{:S(2)}) async-start(), calls=%async_computation.22 | async-start | bytes 2621440 | tf_op jit(solution)/shard_map/reduce_scatter | solution.py:291
  1453.1 246.2 %reduce-scatter.20.cloned.1.call-start = ((), (), s32[]{:S(2)}) async-start(), calls=%async_computation.23 | async-start | bytes 10485760 | tf_op jit(solution)/shard_map/reduce_scatter | solution.py:294
  1461.2 529.7 %reduce-scatter.22.cloned.1.call-start = ((), (), s32[]{:S(2)}) async-start(), calls=%async_computation.25 | async-start | bytes 41943040
  1478.7 804.2 %reduce-scatter.24.cloned.1.call-start = ((), (), s32[]{:S(2)}) async-start(), calls=%async_computation.26 | async-start | bytes 41943040
  1495.7 1078.8 %reduce-scatter.26.cloned.1.call-start = ((), (), s32[]{:S(2)}) async-start(), calls=%async_computation.27 | async-start | bytes 41943040
  1512.7 1214.8 %all-gather.26.cloned.1.call-start = ((), (), s32[]{:S(2)}) async-start(), calls=%async_computation.24 | async-start | bytes 18874368 | tf_op jit(solution)/shard_map/all_gather | solution.py:305
  1532.4 1750.0 %all-reduce.10.cloned.1.call-start = ((), (), s32[]{:S(2)}) async-start(), calls=%async_computation.28 | async-start | bytes 56623104 | tf_op jit(solution)/shard_map/psum | solution.py:306
  (39 other events, 675.9 us)
Sparse Core Ops, SparseCore 0:
  9.9 38.0 all-gather.15
  49.8 35.2 all-gather.13
  87.0 87.5 all-gather.11
  176.3 87.5 all-gather.17
  265.6 297.2 all-gather.19
  564.6 297.2 all-gather.21
  863.6 297.2 all-gather.23
  1448.0 84.3 reduce-scatter.13
  1535.6 35.1 reduce-scatter.15
  1573.7 35.1 reduce-scatter.17
  1612.9 86.4 reduce-scatter.19
  1702.2 288.6 reduce-scatter.21
  1994.2 288.6 reduce-scatter.23
  2285.9 288.6 reduce-scatter.25
  2576.0 151.3 all-gather.25
  2730.9 551.4 all-reduce.9
